TPU v7x, 32 devices: a whole 2x2x4 slice. The times are simulated.
32 devices in a mesh: mem: 16 (over z, y, x), patch: 2 (over core).
Axes of the slice: x: 2, y: 2, z: 4, core: 2. Of those that a mesh axis runs over, the one named last changes fastest.
Arguments:
- state: bfloat16 [3, 1024, 8192], P(None, 'mem', 'patch'), may hold values from -6 to 6
- obs_noise: bfloat16 [1024, 8192], P('mem', 'patch'), may hold values from -6 to 6
- obs_values: float32 [2, 4096], P('patch', 'mem'), may hold values from -6 to 6
- obs_weights: bfloat16 [2, 32, 128, 128], P('patch', 'mem'), may hold values from -1 to 1
- tapers: float32 [8, 128, 128], replicated, may hold values from 0.2 to 1
- pair_source: int32 [2, 32, 4], P('patch', 'mem'), may hold values from 0 to 31, as said below
- pair_taper: int32 [2, 32, 4], P('patch', 'mem'), may hold values from 0 to 7
Outputs:
- analysis: bfloat16 [3, 1024, 8192], P(None, 'mem', 'patch')
Inputs may be any that keep to these rules, and one draw needn't show every extreme that they name: `pair_source`: each listed source lies in the same patch within 2 blocks of its target block; positions beyond the patch's ends are moved to its first or last block.
All inputs are finite; a program needn't handle non-finite values.
Results may differ from a plain program's by a relative error of at most 0.0058.
Values may be sent and summed in bfloat16 or wider, within the bound.
A program may use at most 64 MiB of HBM per device.

v0:
```python
import jax
import jax.numpy as jnp
from jax import lax
from jax.sharding import PartitionSpec as P

MEMBERS = 1024
VARIABLES = 3
BLOCK_CELLS = 128
RADIUS = 2
PAIRS = 4
BLOCKS_DEV = 2


def padded(cells, sides, width):
    for axis, dim in sides:
        count = lax.axis_size(axis)
        ends = count - 1
        head = lax.slice_in_dim(cells, 0, width, axis=dim)
        tail = lax.slice_in_dim(cells, cells.shape[dim] - width, cells.shape[dim], axis=dim)
        cells = jnp.concatenate(
            [
                lax.ppermute(tail, axis, [(i, (i + 1) % count) for i in range(ends)]),
                cells,
                lax.ppermute(head, axis, [((i + 1) % count, i) for i in range(ends)]),
            ],
            axis=dim,
        )
    return cells


def centered(values):
    wide = values.astype(jnp.float32)
    return (wide - jnp.mean(wide, axis=-2, keepdims=True)).astype(jnp.bfloat16)


def on_device(state, obs_noise, obs_values, obs_weights, tapers, pair_source, pair_taper):
    observed, noise_cols = (
        lax.all_to_all(state[0], "mem", split_axis=1, concat_axis=0, tiled=True),
        lax.all_to_all(obs_noise, "mem", split_axis=1, concat_axis=0, tiled=True),
    )
    members = observed.shape[0]
    owned = observed.shape[1]
    anom_first = centered(observed)
    innovation = (
        obs_values[0][None, :] + noise_cols.astype(jnp.float32) - observed.astype(jnp.float32)
    ).astype(jnp.bfloat16)
    weighted = jnp.einsum(
        "nkd,kcd->nkc",
        innovation.reshape(members, BLOCKS_DEV, BLOCK_CELLS),
        obs_weights[0],
        preferred_element_type=jnp.float32,
    )
    weighted = weighted.astype(jnp.bfloat16).reshape(members, owned)
    window = padded(jnp.stack([anom_first, weighted]), (("mem", 2),), RADIUS * BLOCK_CELLS)
    others = lax.all_to_all(state[1:], "mem", split_axis=2, concat_axis=1, tiled=True)
    cell_state = jnp.concatenate([observed[None], others], axis=0)
    anomalies = jnp.concatenate([anom_first[None], centered(others)], axis=0)
    first_block = lax.axis_index("mem") * BLOCKS_DEV
    results = []
    for block in range(BLOCKS_DEV):
        target_anom = anomalies[:, :, block * BLOCK_CELLS : (block + 1) * BLOCK_CELLS]
        slices = []
        taper_tiles = []
        for slot in range(PAIRS):
            offset = (pair_source[0, block, slot] - first_block + RADIUS) * BLOCK_CELLS
            slices.append(lax.dynamic_slice_in_dim(window, offset, BLOCK_CELLS, 2))
            taper_tiles.append(
                lax.dynamic_index_in_dim(tapers, pair_taper[0, block, slot], 0, keepdims=False)
            )
        sources = jnp.concatenate(slices, axis=2)
        taper_row = jnp.concatenate(taper_tiles, axis=1)
        pieces = []
        for variable in range(VARIABLES):
            covariance = lax.dot_general(
                target_anom[variable],
                sources[0],
                (((0,), (0,)), ((), ())),
                preferred_element_type=jnp.float32,
            ) / (MEMBERS - 1)
            localized = (taper_row * covariance).astype(jnp.bfloat16)
            pieces.append(
                lax.dot_general(
                    sources[1],
                    localized,
                    (((1,), (1,)), ((), ())),
                    preferred_element_type=jnp.float32,
                )
            )
        total = jnp.stack(pieces)
        results.append(total)
    increment = jnp.concatenate(results, axis=2)
    updated = (cell_state.astype(jnp.float32) + increment).astype(jnp.bfloat16)
    return lax.all_to_all(updated, "mem", split_axis=1, concat_axis=2, tiled=True)


def solution(mesh):
    placed = (
        P(None, "mem", "patch"),
        P("mem", "patch"),
        P("patch", "mem"),
        P("patch", "mem", None, None),
        P(),
        P("patch", "mem", None),
        P("patch", "mem", None),
    )
    return jax.shard_map(
        on_device, mesh=mesh, in_specs=placed, out_specs=P(None, "mem", "patch"), check_vma=False
    )
```

profile of v0, /device:TPU:0, one launch (start us, length us, event | category | flops | bytes accessed | tf_op | source)
XLA Modules:
  0.0 197.0 jit_solution(13814769640638829721)
XLA Ops:
  0.0 1.1 slice.106
  1.3 1.0 copy.27
  2.2 8.3 %all-to-all-start = ((bf16[64,16,256]{2,0,1:T(8,128)(2,1)}), bf16[64,16,256]{2,0,1:T(8,128)(2,1)S(1)}, u32[]{:S(2)}, u32[]{:S(2)}) async-start(bf16[64,16,256]{2,0,1:T(8,128)(2,1)} %copy.27), calls=%async_computation | async-start | bytes 1048576 | tf_op jit(solution)/shard_map/all_to_all | solution.py:38
  10.6 0.9 copy.48
  11.4 14.2 %all-to-all-done = bf16[64,16,256]{2,0,1:T(8,128)(2,1)S(1)} async-done(((bf16[64,16,256]{2,0,1:T(8,128)(2,1)}), bf16[64,16,256]{2,0,1:T(8,128)(2,1)S(1)}, u32[]{:S(2)}, u32[]{:S(2)}) %all-to-all-start) | async-done | bytes 524320 | tf_op jit(solution)/shard_map/all_to_all | solution.py:38
  25.7 3.9 %all-to-all-start.2 = ((bf16[64,16,256]{2,0,1:T(8,128)(2,1)}), bf16[64,16,256]{2,0,1:T(8,128)(2,1)S(1)}, u32[]{:S(2)}, u32[]{:S(2)}) async-start(bf16[64,16,256]{2,0,1:T(8,128)(2,1)} %bitcast.130), calls=%async_computation.2 | async-start | bytes 1048576 | tf_op jit(solution)/shard_map/all_to_all | solution.py:39
  29.6 1.0 slice.107
  30.7 5.0 %copy.41 = bf16[2,64,4096]{1,0,2:T(2,128)(2,1)S(1)} copy(bf16[2,64,4096]{2,1,0:T(8,128)(2,1)} %slice.107) | data formatting | bytes 2097152
  35.7 2.3 %reshape.67 = bf16[16,2,16384]{2,1,0:T(2,128)(2,1)} reshape(bf16[4096,2,64]{2,1,0:T(2,128)(2,1)S(1)} %bitcast.135) | data formatting | bytes 2097152
  38.0 6.1 %all-to-all-done.2 = bf16[64,16,256]{2,0,1:T(8,128)(2,1)S(1)} async-done(((bf16[64,16,256]{2,0,1:T(8,128)(2,1)}), bf16[64,16,256]{2,0,1:T(8,128)(2,1)S(1)}, u32[]{:S(2)}, u32[]{:S(2)}) %all-to-all-start.2) | async-done | bytes 524320 | tf_op jit(solution)/shard_map/all_to_all | solution.py:39
  44.0 0.8 copy-done.8
  44.8 3.9 %all-to-all-start.1 = ((bf16[16,2,16384]{2,1,0:T(2,128)(2,1)}), bf16[16,2,16384]{2,1,0:T(2,128)(2,1)S(1)}, u32[]{:S(2)}, u32[]{:S(2)}) async-start(bf16[16,2,16384]{2,1,0:T(2,128)(2,1)} %reshape.67), calls=%async_computation.1 | async-start | bytes 2097152 | tf_op jit(solution)/shard_map/all_to_all | solution.py:55
  48.7 1.1 bitcast_convert_fusion
  49.8 1.7 reshape.66
  51.6 1.1 convert_bitcast_fusion
  52.7 2.7 %reshape.65 = f32[1024,2,128]{2,1,0:T(2,128)} reshape(f32[16,64,256]{2,1,0:T(8,128)} %convert_bitcast_fusion) | data formatting | bytes 2097152 | tf_op jit(solution)/shard_map/convert_element_type | solution.py:45
  55.4 1.8 subtract_convert_fusion.1
  57.2 0.3 convolution_convert_fusion
  57.5 0.2 copy.35
  58.0 0.8 copy-done.1
  58.8 1.1 pad_maximum_fusion.3
  59.9 1.3 collective-permute-start.1
  61.2 5.5 %collective-permute-start = (bf16[2,1024,256]{2,1,0:T(8,128)(2,1)}, bf16[2,1024,256]{2,1,0:T(8,128)(2,1)}, u32[]{:S(2)}, u32[]{:S(2)}) collective-permute-start(bf16[2,1024,256]{2,1,0:T(8,128)(2,1)} %pad_maximum_fusion.3), channel_id=1, source_target_pairs={{0,2},{2,4},{4,6},{6,8},{8,10},{10,12},{12,14},{14,16},{16,18},{18... | collective-permute-start | bytes 3145736 | tf_op jit(solution)/shard_map/ppermute | solution.py:22
  66.7 0.7 fusion.35
  72.4 0.7 fusion.34
  87.9 0.7 dynamic-slice_bitcast_fusion.7
  88.6 1.0 copy.31
  89.6 1.3 reshape.68
  91.0 2.4 %copy.39 = bf16[2,64,16,256]{3,2,1,0:T(8,128)(2,1)} copy(bf16[2,64,16,256]{1,0,3,2:T(2,128)(2,1)S(1)} %bitcast.131) | data formatting | bytes 2097152 | tf_op jit(solution)/shard_map/all_to_all | solution.py:55
  93.3 1.4 copy.40
  94.8 1.3 copy.32
  96.1 0.2 convert_reduce_fusion
  96.3 1.3 subtract_convert_fusion
  97.6 14.6 %collective-permute-done = bf16[2,1024,256]{2,1,0:T(8,128)(2,1)} collective-permute-done((bf16[2,1024,256]{2,1,0:T(8,128)(2,1)}, bf16[2,1024,256]{2,1,0:T(8,128)(2,1)}, u32[]{:S(2)}, u32[]{:S(2)}) %collective-permute-start) | collective-permute-done | bytes 1048608 | tf_op jit(solution)/shard_map/ppermute | solution.py:22
  112.2 1.6 pad_maximum_fusion
  113.9 0.9 constant_dynamic-slice_fusion.7
  114.8 1.6 pad_maximum_fusion.1
  116.3 3.1 %convolution_bitcast_fusion = f32[1,1024,128]{1,2,0:T(8,128)S(1)} fusion(bf16[2,1024,512]{2,1,0:T(8,128)(2,1)} %get-tuple-element.38, bf16[2,1024,256]{2,1,0:T(8,128)(2,1)} %subtract_convert_fusion, f32[128,128]{1,0:T(8,128)} %get-tuple-element.19, f32[128,128]{1,0:T(8,128)} %get-tuple-element.20, f32[128,128]{1,0:T(8,128)S(1)} %get-tuple-element.14, ...), kind=kOutput, calls=%fused_computation.8 | convolution fusion | flops 268828672 | bytes 3145728 | tf_op jit(solution)/shard_map/dot_general | solution.py:82
  119.5 3.2 %convolution_bitcast_fusion.1 = f32[1,1024,128]{1,2,0:T(8,128)} fusion(bf16[2,1024,512]{2,1,0:T(8,128)(2,1)} %get-tuple-element.38, bf16[2,1024,256]{2,1,0:T(8,128)(2,1)} %subtract_convert_fusion, f32[128,128]{1,0:T(8,128)} %get-tuple-element.19, f32[128,128]{1,0:T(8,128)} %get-tuple-element.20, f32[128,128]{1,0:T(8,128)S(1)} %get-tuple-element.14, ...), kind=kOutput, calls=%fused_computation.9 | convolution fusion | flops 268828672 | bytes 3145728 | tf_op jit(solution)/shard_map/dot_general | solution.py:82
  122.7 3.1 %convolution_bitcast_fusion.2 = f32[1,1024,128]{1,2,0:T(8,128)} fusion(bf16[2,1024,512]{2,1,0:T(8,128)(2,1)} %get-tuple-element.38, bf16[1,1024,256]{2,1,0:T(8,128)(2,1)S(1)} %copy-done.2, f32[128,128]{1,0:T(8,128)} %get-tuple-element.19, f32[128,128]{1,0:T(8,128)} %get-tuple-element.20, f32[128,128]{1,0:T(8,128)S(1)} %get-tuple-element.14, ...), kind=kOutput, calls=%fused_computation.10 | convolution fusion | flops 268828672 | bytes 3145728 | tf_op jit(solution)/shard_map/dot_general | solution.py:82
  125.7 2.5 %convolution_bitcast_fusion.3 = f32[1,1024,128]{1,2,0:T(8,128)} fusion(bf16[2,1024,512]{2,1,0:T(8,128)(2,1)S(1)} %get-tuple-element.37, bf16[2,1024,256]{2,1,0:T(8,128)(2,1)} %subtract_convert_fusion, f32[128,128]{1,0:T(8,128)S(1)} %get-tuple-element.16, f32[128,128]{1,0:T(8,128)S(1)} %get-tuple-element.17, f32[128,128]{1,0:T(8,128)S(1)} %get-tuple-element.18, ...), kind=kOutput, calls=%fused_computation.11 | convolution fusion | flops 268828672 | bytes 3145728 | tf_op jit(solution)/shard_map/dot_general | solution.py:82
  128.2 2.5 %convolution_bitcast_fusion.4 = f32[1,1024,128]{1,2,0:T(8,128)} fusion(bf16[2,1024,512]{2,1,0:T(8,128)(2,1)S(1)} %get-tuple-element.37, bf16[2,1024,256]{2,1,0:T(8,128)(2,1)} %subtract_convert_fusion, f32[128,128]{1,0:T(8,128)S(1)} %get-tuple-element.16, f32[128,128]{1,0:T(8,128)S(1)} %get-tuple-element.17, f32[128,128]{1,0:T(8,128)S(1)} %get-tuple-element.18, ...), kind=kOutput, calls=%fused_computation.12 | convolution fusion | flops 268828672 | bytes 3145728 | tf_op jit(solution)/shard_map/dot_general | solution.py:82
  130.7 3.2 %convolution_bitcast_fusion.5 = f32[1,1024,128]{1,2,0:T(8,128)} fusion(bf16[2,1024,512]{2,1,0:T(8,128)(2,1)} %copy-done.10, bf16[1,1024,256]{2,1,0:T(8,128)(2,1)S(1)} %copy-done.2, f32[128,128]{1,0:T(8,128)S(1)} %get-tuple-element.16, f32[128,128]{1,0:T(8,128)S(1)} %get-tuple-element.17, f32[128,128]{1,0:T(8,128)S(1)} %get-tuple-element.18, ...), kind=kOutput, calls=%fused_computation.13 | convolution fusion | flops 268828672 | bytes 3145728 | tf_op jit(solution)/shard_map/dot_general | solution.py:82
  133.9 2.7 %fusion = bf16[3,1024,256]{1,2,0:T(8,128)(2,1)} fusion(f32[1,1024,128]{1,2,0:T(8,128)S(1)} %convolution_bitcast_fusion, f32[1,1024,128]{1,2,0:T(8,128)S(1)} %copy-done.12, f32[1,1024,128]{1,2,0:T(8,128)} %convolution_bitcast_fusion.2, f32[1,1024,128]{1,2,0:T(8,128)} %convolution_bitcast_fusion.3, f32[1,1024,128]{1,2,0:T(8,128)} %convolution_bitcast_fusion.4, ...), kind=kLoop, calls=%fused_computation.2 | loop fusion | flops 7077888 | bytes 6291456 | tf_op jit(solution)/shard_map/convert_element_type | solution.py:92
  136.6 2.9 %copy.36 = bf16[3,1024,256]{2,0,1:T(4,128)(2,1)S(1)} copy(bf16[3,1024,256]{1,2,0:T(8,128)(2,1)} %fusion) | data formatting | bytes 3145728 | tf_op jit(solution)/shard_map/convert_element_type | solution.py:92
  139.6 55.9 %all_to_all.65 = bf16[3,1024,256]{2,0,1:T(4,128)(2,1)S(1)} all-to-all(bf16[3,1024,256]{2,0,1:T(4,128)(2,1)S(1)} %copy.36), channel_id=1, replica_groups=mesh['mem'=16,'patch'=2] {'mem'}, dimensions={1} | all-to-all | bytes 3145728 | tf_op jit(solution)/shard_map/all_to_all | solution.py:93
  195.4 0.2 copy.37
  195.7 1.3 copy.43
  (41 shorter events, 0.5 us)
Async XLA Ops:
  0.0 57.1 %copy-start = (bf16[1,2,128,128]{3,2,1,0:T(8,128)(2,1)S(1)}, bf16[1,2,128,128]{3,2,1,0:T(8,128)(2,1)}, u32[]{:S(2)}) copy-start(bf16[1,2,128,128]{3,2,1,0:T(8,128)(2,1)} %param.10) | copy-start | bytes 196612
  0.0 10.6 %copy-start.13 = (bf16[64,4096]{1,0:T(8,128)(2,1)S(1)}, bf16[64,4096]{1,0:T(8,128)(2,1)}, u32[]{:S(2)}) copy-start(bf16[64,4096]{1,0:T(8,128)(2,1)} %param.8) | copy-start | bytes 1572868
  1.3 28.4 %copy-start.11 = (bf16[3,64,4096]{2,1,0:T(8,128)(2,1)S(1)}, bf16[3,64,4096]{2,1,0:T(8,128)(2,1)}, u32[]{:S(2)}) copy-start(bf16[3,64,4096]{2,1,0:T(8,128)(2,1)} %param.7) | copy-start | bytes 4718596
  2.2 23.4 %all-to-all-start = ((bf16[64,16,256]{2,0,1:T(8,128)(2,1)}), bf16[64,16,256]{2,0,1:T(8,128)(2,1)S(1)}, u32[]{:S(2)}, u32[]{:S(2)}) async-start(bf16[64,16,256]{2,0,1:T(8,128)(2,1)} %copy.27), calls=%async_computation | async-start | bytes 1048576 | tf_op jit(solution)/shard_map/all_to_all | solution.py:38
  25.7 18.4 %all-to-all-start.2 = ((bf16[64,16,256]{2,0,1:T(8,128)(2,1)}), bf16[64,16,256]{2,0,1:T(8,128)(2,1)S(1)}, u32[]{:S(2)}, u32[]{:S(2)}) async-start(bf16[64,16,256]{2,0,1:T(8,128)(2,1)} %bitcast.130), calls=%async_computation.2 | async-start | bytes 1048576 | tf_op jit(solution)/shard_map/all_to_all | solution.py:39
  44.0 0.8 copy-start.8
  44.8 44.8 %all-to-all-start.1 = ((bf16[16,2,16384]{2,1,0:T(2,128)(2,1)}), bf16[16,2,16384]{2,1,0:T(2,128)(2,1)S(1)}, u32[]{:S(2)}, u32[]{:S(2)}) async-start(bf16[16,2,16384]{2,1,0:T(2,128)(2,1)} %reshape.67), calls=%async_computation.1 | async-start | bytes 2097152 | tf_op jit(solution)/shard_map/all_to_all | solution.py:55
  48.7 2.8 %copy-start.9 = (bf16[64,16,256]{2,0,1:T(8,128)(2,1)S(1)}, bf16[64,16,256]{2,0,1:T(8,128)(2,1)}, u32[]{:S(2)}) copy-start(bf16[64,16,256]{2,0,1:T(8,128)(2,1)} %copy-done.8) | copy-start | bytes 1572868
  51.6 3.8 %copy-start.17 = (f32[1,256]{1,0:T(1,128)S(1)}, f32[1,256]{1,0:T(1,128)}, u32[]{:S(2)}) copy-start(f32[1,256]{1,0:T(1,128)} %param.9) | copy-start | bytes 3076
  57.7 30.9 %copy-start.3 = (bf16[1,1024,256]{2,1,0:T(8,128)(2,1)}, bf16[1,1024,256]{2,1,0:T(8,128)(2,1)S(1)}, u32[]{:S(2)}) copy-start(bf16[1,1024,256]{2,1,0:T(8,128)(2,1)S(1)} %copy.35) | copy-start | bytes 1572868
  57.7 9.0 %copy-start.15 = (s32[1,2,4]{2,1,0:T(2,128)S(1)}, s32[1,2,4]{2,1,0:T(2,128)}, u32[]{:S(2)}) copy-start(s32[1,2,4]{2,1,0:T(2,128)} %param.12) | copy-start | bytes 100
  57.7 14.7 %copy-start.16 = (s32[1,2,4]{2,1,0:T(2,128)S(1)}, s32[1,2,4]{2,1,0:T(2,128)}, u32[]{:S(2)}) copy-start(s32[1,2,4]{2,1,0:T(2,128)} %param.13) | copy-start | bytes 100
  57.7 30.2 %copy-start.14 = (f32[8,128,128]{2,1,0:T(8,128)S(1)}, f32[8,128,128]{2,1,0:T(8,128)}, u32[]{:S(2)}) copy-start(f32[8,128,128]{2,1,0:T(8,128)} %param.11) | copy-start | bytes 1572868
  58.0 0.8 copy-start.1
  59.9 37.7 %collective-permute-start.1 = (bf16[2,1024,256]{2,1,0:T(8,128)(2,1)}, bf16[2,1024,256]{2,1,0:T(8,128)(2,1)}, u32[]{:S(2)}, u32[]{:S(2)}) collective-permute-start(bf16[2,1024,256]{2,1,0:T(8,128)(2,1)} %pad_maximum_fusion.3), channel_id=1, source_target_pairs={{2,0},{4,2},{6,4},{8,6},{10,8},{12,10},{14,12},{16,14},{18,16},{20... | collective-permute-start | bytes 3145736 | tf_op jit(solution)/shard_map/ppermute | solution.py:24
  61.2 51.1 %collective-permute-start = (bf16[2,1024,256]{2,1,0:T(8,128)(2,1)}, bf16[2,1024,256]{2,1,0:T(8,128)(2,1)}, u32[]{:S(2)}, u32[]{:S(2)}) collective-permute-start(bf16[2,1024,256]{2,1,0:T(8,128)(2,1)} %pad_maximum_fusion.3), channel_id=1, source_target_pairs={{0,2},{2,4},{4,6},{6,8},{8,10},{10,12},{12,14},{14,16},{16,18},{18... | collective-permute-start | bytes 3145736 | tf_op jit(solution)/shard_map/ppermute | solution.py:22
  94.8 1.3 copy-start.5
  96.1 16.1 %copy-start.2 = (bf16[1,1024,256]{2,1,0:T(8,128)(2,1)S(1)}, bf16[1,1024,256]{2,1,0:T(8,128)(2,1)}, u32[]{:S(2)}) copy-start(bf16[1,1024,256]{2,1,0:T(8,128)(2,1)} %copy-done.1) | copy-start | bytes 1572868
  96.1 16.1 %copy-start.4 = (bf16[1,1024,256]{2,1,0:T(8,128)(2,1)S(1)}, bf16[1,1024,256]{2,1,0:T(8,128)(2,1)}, u32[]{:S(2)}) copy-start(bf16[1,1024,256]{2,1,0:T(8,128)(2,1)} %copy-done.3) | copy-start | bytes 1572868
  116.3 11.9 %copy-start.10 = (bf16[2,1024,512]{2,1,0:T(8,128)(2,1)}, bf16[2,1024,512]{2,1,0:T(8,128)(2,1)S(1)}, u32[]{:S(2)}) copy-start(bf16[2,1024,512]{2,1,0:T(8,128)(2,1)S(1)} %get-tuple-element.37) | copy-start | bytes 6291460
  130.7 3.2 %copy-start.6 = (bf16[2,1024,256]{1,2,0:T(8,128)(2,1)S(1)}, bf16[2,1024,256]{1,2,0:T(8,128)(2,1)}, u32[]{:S(2)}) copy-start(bf16[2,1024,256]{1,2,0:T(8,128)(2,1)} %copy.32) | copy-start | bytes 3145732
  130.7 3.2 %copy-start.7 = (bf16[1,1024,256]{1,2,0:T(8,128)(2,1)S(1)}, bf16[1,1024,256]{1,2,0:T(8,128)(2,1)}, u32[]{:S(2)}) copy-start(bf16[1,1024,256]{1,2,0:T(8,128)(2,1)} %copy.31) | copy-start | bytes 1572868
  130.7 3.2 %copy-start.12 = (f32[1,1024,128]{1,2,0:T(8,128)S(1)}, f32[1,1024,128]{1,2,0:T(8,128)}, u32[]{:S(2)}) copy-start(f32[1,1024,128]{1,2,0:T(8,128)} %convolution_bitcast_fusion.1) | copy-start | bytes 1572868
where the time goes:
time: 198 us; the launch traced here: 197 us
  blocking collectives  55.9 us (28%)
  waiting for transfers between devices  34.9 us (18%)
  local copies, waits for them, and re-layouts  32.6 us (16%)
  starting transfers between devices  23 us (12%)
  between operations  20.1 us (10%)
  matrix products  17.8 us (9%)
  other arithmetic  12.7 us (6%)
    all_to_all x1, blocking collectives, on_device(): lax.all_to_all(updated, 'mem', split_axis=1, concat_axis=2, tiled=True)  55.9 us
    dot_general x6, matrix products, on_device(): lax.dot_general(sources[1], localized, (((1,), (1,)), ((), ())), preferre...  17.5 us
    ppermute x1, waiting for transfers between devices, padded(): lax.ppermute(tail, axis, [(i, (i + 1) % count) for i in range(ends)])  14.6 us
    all_to_all x1, waiting for transfers between devices, on_device(): lax.all_to_all(state[0], 'mem', split_axis=1, concat_axis=0, tiled=True)  14.2 us
    unnamed x40, local copies, waits for them, and re-layouts  10.4 us
    all_to_all x1, starting transfers between devices, on_device(): lax.all_to_all(state[0], 'mem', split_axis=1, concat_axis=0, tiled=True)  8.34 us
    all_to_all x1, waiting for transfers between devices, on_device(): lax.all_to_all(obs_noise, 'mem', split_axis=1, concat_axis=0, tiled=True)  6.07 us
    ppermute x1, starting transfers between devices, padded(): lax.ppermute(tail, axis, [(i, (i + 1) % count) for i in range(ends)])  5.55 us
  transfers between devices with their start and end apart: 5, of which 3 were waited for; matrix products, arithmetic and copies ran while one was open for 15% of the time, Pallas kernels for 0%

commit v1 on v0

v1 whole, which is shorter than its diff:
```python
import functools

import jax
import jax.numpy as jnp
from jax import lax
from jax.experimental import pallas as pl
from jax.experimental.pallas import tpu as pltpu
from jax.sharding import PartitionSpec as P

RADIUS = 2
MESH = pl.DeviceIdType.MESH


def kernel(
    n,
    state, noise, obs_values, obs_weights, tapers, pair_source, pair_taper,
    out,
    rin, win_at, win_w, anom, local_t, taper_t, outbuf,
    in_send, in_recv, local_sem, halo_send, halo_recv, out_send, out_recv,
):
    me = lax.axis_index("mem")
    part = lax.axis_index("patch")
    variables, rows, _ = state.shape
    members, owned = rin.shape[1], rin.shape[2]
    blocks = obs_weights.shape[1]
    size = obs_weights.shape[2]
    pairs = pair_source.shape[2]
    kinds = rin.shape[0]
    wide = variables * size

    barrier = pltpu.get_barrier_semaphore()

    def greet(k, _):
        peer = lax.rem(me + k, n)
        pl.semaphore_signal(barrier, inc=1, device_id=(peer, part), device_id_type=MESH)
        return 0

    lax.fori_loop(1, n, greet, 0)

    def source(kind, owner):
        columns = pl.ds(pl.multiple_of(owner * owned, owned), owned)
        return noise.at[:, columns] if kind == 1 else state.at[max(kind - 1, 0), :, columns]

    my_rows = pl.ds(pl.multiple_of(me * rows, rows), rows)
    locals_ = [
        pltpu.make_async_copy(source(kind, me), rin.at[kind, my_rows], local_sem.at[kind])
        for kind in range(kinds)
    ]
    for copy in locals_:
        copy.start()
    pl.semaphore_wait(barrier, n - 1)

    for kind in range(kinds):
        def send(k, _, kind=kind):
            peer = lax.rem(me + k, n)
            pltpu.make_async_remote_copy(
                src_ref=source(kind, peer),
                dst_ref=rin.at[kind, my_rows],
                send_sem=in_send.at[kind],
                recv_sem=in_recv.at[kind],
                device_id=(peer, part),
                device_id_type=MESH,
            ).start()
            return 0

        lax.fori_loop(1, n, send, 0)

    for k in range(tapers.shape[0]):
        taper_t[k] = tapers[k].T * (1.0 / (members - 1))

    remote_rows = (n - 1) * rows

    def arrived(kind):
        locals_[kind].wait()
        block = rin.at[kind, pl.ds(0, remote_rows)]
        pltpu.make_async_copy(block, block, in_recv.at[kind]).wait()

    def centered(kind):
        values = rin[kind].astype(jnp.float32)
        center = jnp.sum(values, axis=0, keepdims=True) * (1.0 / members)
        return (values - center).astype(jnp.bfloat16)

    arrived(0)
    first = centered(0)
    for b in range(blocks):
        tile = first[:, b * size : (b + 1) * size]
        anom[b, :, 0:size] = tile
        win_at[RADIUS + b] = tile.T

    own = pl.ds(RADIUS, blocks)
    halo = []

    def exchange(window, index):
        left = pltpu.make_async_remote_copy(
            src_ref=window.at[own],
            dst_ref=window.at[pl.ds(RADIUS + blocks, blocks)],
            send_sem=halo_send.at[index, 0],
            recv_sem=halo_recv.at[index, 0],
            device_id=(jnp.maximum(me - 1, 0), part),
            device_id_type=MESH,
        )
        right = pltpu.make_async_remote_copy(
            src_ref=window.at[own],
            dst_ref=window.at[pl.ds(0, blocks)],
            send_sem=halo_send.at[index, 1],
            recv_sem=halo_recv.at[index, 1],
            device_id=(jnp.minimum(me + 1, n - 1), part),
            device_id_type=MESH,
        )

        @pl.when(me > 0)
        def _():
            left.start()

        @pl.when(me < n - 1)
        def _():
            right.start()

        halo.append((left, right))

    exchange(win_at, 0)
    arrived(1)
    innovation = (
        obs_values[...] + rin[1].astype(jnp.float32) - rin[0].astype(jnp.float32)
    ).astype(jnp.bfloat16)
    for b in range(blocks):
        win_w[RADIUS + b] = lax.dot_general(
            innovation[:, b * size : (b + 1) * size],
            obs_weights[0, b],
            (((1,), (1,)), ((), ())),
            preferred_element_type=jnp.float32,
        ).astype(jnp.bfloat16)
    exchange(win_w, 1)

    for kind in range(2, kinds):
        arrived(kind)
        values = centered(kind)
        for b in range(blocks):
            anom[b, :, (kind - 1) * size : kind * size] = values[:, b * size : (b + 1) * size]

    def landed(index):
        left, right = halo[index]

        @pl.when(me > 0)
        def _():
            left.wait_send()
            right.wait_recv()

        @pl.when(me < n - 1)
        def _():
            right.wait_send()
            left.wait_recv()

    landed(0)
    base = me * blocks - RADIUS

    def slot(b, j):
        return jnp.clip(pair_source[0, b, j] - base, 0, win_at.shape[0] - 1)

    for b in range(blocks):
        def pair(j, _, b=b):
            at = win_at[slot(b, j)]
            covariance = jnp.dot(at, anom[b], preferred_element_type=jnp.float32)
            taper = taper_t[pair_taper[0, b, j]]
            local_t[b, pl.ds(pl.multiple_of(j * size, size), size), :] = (
                covariance * jnp.concatenate([taper] * variables, axis=1)
            ).astype(jnp.bfloat16)
            return 0

        lax.fori_loop(0, pairs, pair, 0)

    landed(1)
    chunk = 256
    chunks = members // chunk
    per = chunk // rows
    mine = pl.ds(pl.multiple_of(me * owned, owned), owned)

    def answer(i, _):
        at = lax.rem(i + me // per, chunks)
        here = pl.ds(pl.multiple_of(at * chunk, chunk), chunk)
        for b in range(blocks):
            weights = jnp.concatenate(
                [win_w[slot(b, j), here, :] for j in range(pairs)], axis=1
            )
            increment = jnp.dot(weights, local_t[b], preferred_element_type=jnp.float32)
            for v in range(variables):
                kind = v + 1 if v else 0
                part_of = slice(b * size, (b + 1) * size)
                outbuf[v, here, part_of] = (
                    rin[kind, here, part_of].astype(jnp.float32)
                    + increment[:, v * size : (v + 1) * size]
                ).astype(jnp.bfloat16)

        def give(k, _):
            peer = at * per + lax.rem(k + me, per)
            theirs = pl.ds(pl.multiple_of(peer * rows, rows), rows)

            @pl.when(peer != me)
            def _():
                pltpu.make_async_remote_copy(
                    src_ref=outbuf.at[:, theirs, :],
                    dst_ref=out.at[:, :, mine],
                    send_sem=out_send,
                    recv_sem=out_recv,
                    device_id=(peer, part),
                    device_id_type=MESH,
                ).start()

            return 0

        lax.fori_loop(0, per, give, 0)
        return 0

    lax.fori_loop(0, chunks, answer, 0)
    keep = pltpu.make_async_copy(outbuf.at[:, my_rows, :], out.at[:, :, mine], local_sem.at[kinds])
    keep.start()
    keep.wait()
    for kind in range(kinds):
        block = rin.at[kind, pl.ds(0, remote_rows)]
        pltpu.make_async_copy(block, block, in_send.at[kind]).wait()
    block = outbuf.at[:, pl.ds(0, remote_rows), :]
    pltpu.make_async_copy(block, block, out_send).wait()
    pltpu.make_async_copy(block, block, out_recv).wait()


def on_device(n, state, obs_noise, obs_values, obs_weights, tapers, pair_source, pair_taper):
    variables, rows, cells = state.shape
    members = rows * n
    owned = cells // n
    blocks, size = obs_weights.shape[1], obs_weights.shape[2]
    pairs = pair_source.shape[2]
    window = blocks + 2 * RADIUS
    anywhere = pl.BlockSpec(memory_space=pl.ANY)
    vmem = pl.BlockSpec(memory_space=pltpu.VMEM)
    smem = pl.BlockSpec(memory_space=pltpu.SMEM)
    kinds = variables + 1
    return pl.pallas_call(
        functools.partial(kernel, n),
        out_shape=jax.ShapeDtypeStruct(state.shape, state.dtype),
        in_specs=[anywhere, anywhere, vmem, vmem, vmem, smem, smem],
        out_specs=anywhere,
        scratch_shapes=[
            pltpu.VMEM((kinds, members, owned), jnp.bfloat16),
            pltpu.VMEM((window, size, members), jnp.bfloat16),
            pltpu.VMEM((window, members, size), jnp.bfloat16),
            pltpu.VMEM((blocks, members, variables * size), jnp.bfloat16),
            pltpu.VMEM((blocks, pairs * size, variables * size), jnp.bfloat16),
            pltpu.VMEM(tapers.shape, jnp.float32),
            pltpu.VMEM((variables, members, owned), jnp.bfloat16),
            pltpu.SemaphoreType.DMA((kinds,)),
            pltpu.SemaphoreType.DMA((kinds,)),
            pltpu.SemaphoreType.DMA((kinds + 1,)),
            pltpu.SemaphoreType.DMA((2, 2)),
            pltpu.SemaphoreType.DMA((2, 2)),
            pltpu.SemaphoreType.DMA,
            pltpu.SemaphoreType.DMA,
        ],
        compiler_params=pltpu.CompilerParams(collective_id=0, has_side_effects=True),
    )(state, obs_noise, obs_values, obs_weights, tapers, pair_source, pair_taper)


def solution(mesh):
    placed = (
        P(None, "mem", "patch"),
        P("mem", "patch"),
        P("patch", "mem"),
        P("patch", "mem", None, None),
        P(),
        P("patch", "mem", None),
        P("patch", "mem", None),
    )
    return jax.shard_map(
        functools.partial(on_device, mesh.shape["mem"]),
        mesh=mesh,
        in_specs=placed,
        out_specs=P(None, "mem", "patch"),
        check_vma=False,
    )
```

time: 198 us -> 123 us (0.62)
  the two profiles are of different devices: /device:TPU:0 before, /device:TPU:29 now
where the time goes in v1:
time: 123 us
  Pallas kernels  121 us (98%)
  local copies, waits for them, and re-layouts  2.7 us (2%)
    pallas_call x1, Pallas kernels, on_device(): pl.pallas_call(functools.partial(kernel, n), out_shape=jax.ShapeDtypeStru...  121 us
    unnamed x1, local copies, waits for them, and re-layouts  2.7 us

profile of v1, /device:TPU:29, one launch (start us, length us, event | category | flops | bytes accessed | tf_op | source)
XLA Modules:
  0.0 123.3 jit_solution(3564139296639074752)
XLA Ops:
  0.0 120.6 %shard_map.73 = bf16[3,64,4096]{2,1,0:T(8,128)(2,1)} custom-call(bf16[3,64,4096]{2,1,0:T(8,128)(2,1)} %state.1, bf16[64,4096]{1,0:T(8,128)(2,1)} %noise.1, f32[1,256]{1,0:T(1,128)} %obs_values.1, bf16[1,2,128,128]{3,2,1,0:T(8,128)(2,1)} %obs_weights.1, f32[8,128,128]{2,1,0:T(8,128)} %tapers.1, s32[1,2,4]{2,1,0:T(2,128)} %pair_source.1, s32[1,2,4]{2,1,0:T(2,128)} %pair_taper.1), custom_call_target="tpu_custom_call" | custom-call | tf_op jit(solution)/shard_map/pallas_call | solution.py:237
  120.6 2.7 %copy.9 = bf16[3,64,4096]{2,1,0:T(8,128)(2,1)} copy(bf16[3,64,4096]{2,1,0:T(8,128)(2,1)} %shard_map.73) | data formatting | bytes 3145728

commit v2 on v1

v2 whole, which is shorter than its diff:
```python
import functools

import jax
import jax.numpy as jnp
from jax import lax
from jax.experimental import pallas as pl
from jax.experimental.pallas import tpu as pltpu
from jax.sharding import PartitionSpec as P

RADIUS = 2
MESH = pl.DeviceIdType.MESH


def gray(q):
    return q + (q // 2) * (1 - 2 * (q % 2))


def device_of(rank, part):
    level, q = rank // 4, rank % 4
    q = q + (level % 2) * (3 - 2 * q)
    spot = gray(q)
    return level * 4 + spot + (part % 2) * (3 - 2 * spot)


def rank_of(device, part):
    level, spot = device // 4, device % 4
    spot = spot + (part % 2) * (3 - 2 * spot)
    q = gray(spot)
    return level * 4 + q + (level % 2) * (3 - 2 * q)


def kernel(
    n,
    state, noise, obs_values, obs_weights, tapers, pair_source, pair_taper,
    out,
    rin, win_at, win_w, anom, local_t, taper_in, taper_t, outbuf, weights_in, values_in, source_in, choice_in,
    in_send, in_recv, local_sem, halo_send, halo_recv, out_send, out_recv, small_send, small_recv,
):
    me = lax.axis_index("mem")
    part = lax.axis_index("patch")
    variables, rows, _ = state.shape
    members, owned = rin.shape[1], rin.shape[2]
    blocks, size, _ = weights_in.shape
    pairs = source_in.shape[1]
    kinds = rin.shape[0]
    rank = rank_of(me, part)

    barrier = pltpu.get_barrier_semaphore()

    def greet(k, _):
        peer = lax.rem(me + k, n)
        pl.semaphore_signal(barrier, inc=1, device_id=(peer, part), device_id_type=MESH)
        return 0

    lax.fori_loop(1, n, greet, 0)

    def source(kind, owner):
        columns = pl.ds(pl.multiple_of(owner * owned, owned), owned)
        return noise.at[:, columns] if kind == 1 else state.at[max(kind - 1, 0), :, columns]

    my_rows = pl.ds(pl.multiple_of(me * rows, rows), rows)
    locals_ = [
        pltpu.make_async_copy(source(kind, rank), rin.at[kind, my_rows], local_sem.at[kind])
        for kind in range(kinds)
    ]
    for copy in locals_:
        copy.start()
    taper_copy = pltpu.make_async_copy(tapers, taper_in, local_sem.at[kinds])
    taper_copy.start()
    pl.semaphore_wait(barrier, n - 1)

    def send_kind(kind):
        def send(k, _):
            peer = lax.rem(me + k, n)
            pltpu.make_async_remote_copy(
                src_ref=source(kind, rank_of(peer, part)),
                dst_ref=rin.at[kind, my_rows],
                send_sem=in_send.at[kind],
                recv_sem=in_recv.at[kind],
                device_id=(peer, part),
                device_id_type=MESH,
            ).start()
            return 0

        lax.fori_loop(1, n, send, 0)

    send_kind(0)
    keeper = device_of(me, part)
    small = [
        (obs_weights.at[0], weights_in),
        (obs_values, values_in),
        (pair_source.at[0], source_in),
        (pair_taper.at[0], choice_in),
    ]

    def small_remote(i):
        return pltpu.make_async_remote_copy(
            src_ref=small[i][0],
            dst_ref=small[i][1],
            send_sem=small_send.at[i],
            recv_sem=small_recv.at[i],
            device_id=(keeper, part),
            device_id_type=MESH,
        )

    def small_local(i):
        return pltpu.make_async_copy(small[i][0], small[i][1], small_recv.at[i])

    @pl.when(keeper != me)
    def _():
        for i in range(len(small)):
            small_remote(i).start()

    @pl.when(keeper == me)
    def _():
        for i in range(len(small)):
            small_local(i).start()

    send_kind(1)

    taper_copy.wait()
    for k in range(tapers.shape[0]):
        taper_t[k] = taper_in[k].T * (1.0 / (members - 1))

    remote_rows = (n - 1) * rows

    def arrived(kind):
        locals_[kind].wait()
        block = rin.at[kind, pl.ds(0, remote_rows)]
        pltpu.make_async_copy(block, block, in_recv.at[kind]).wait()

    def centered(kind):
        values = rin[kind].astype(jnp.float32)
        center = jnp.sum(values, axis=0, keepdims=True) * (1.0 / members)
        return (values - center).astype(jnp.bfloat16)

    own = pl.ds(RADIUS, blocks)
    halo = []

    def exchange(window, index):
        left = pltpu.make_async_remote_copy(
            src_ref=window.at[own],
            dst_ref=window.at[pl.ds(RADIUS + blocks, blocks)],
            send_sem=halo_send.at[index, 0],
            recv_sem=halo_recv.at[index, 0],
            device_id=(device_of(jnp.maximum(rank - 1, 0), part), part),
            device_id_type=MESH,
        )
        right = pltpu.make_async_remote_copy(
            src_ref=window.at[own],
            dst_ref=window.at[pl.ds(0, blocks)],
            send_sem=halo_send.at[index, 1],
            recv_sem=halo_recv.at[index, 1],
            device_id=(device_of(jnp.minimum(rank + 1, n - 1), part), part),
            device_id_type=MESH,
        )

        @pl.when(rank > 0)
        def _():
            left.start()

        @pl.when(rank < n - 1)
        def _():
            right.start()

        halo.append((left, right))

    def landed(index):
        left, right = halo[index]

        @pl.when(rank > 0)
        def _():
            left.wait_send()
            right.wait_recv()

        @pl.when(rank < n - 1)
        def _():
            right.wait_send()
            left.wait_recv()

    arrived(0)
    first = centered(0)
    anom[0] = first
    for b in range(blocks):
        win_at[RADIUS + b] = first[:, b * size : (b + 1) * size].T
    exchange(win_at, 0)
    send_kind(2)

    @pl.when(keeper != me)
    def _():
        for i in range(len(small)):
            small_remote(i).wait()

    @pl.when(keeper == me)
    def _():
        for i in range(len(small)):
            small_local(i).wait()

    arrived(1)
    innovation = (
        values_in[...] + rin[1].astype(jnp.float32) - rin[0].astype(jnp.float32)
    ).astype(jnp.bfloat16)
    for b in range(blocks):
        win_w[RADIUS + b] = lax.dot_general(
            innovation[:, b * size : (b + 1) * size],
            weights_in[b],
            (((1,), (1,)), ((), ())),
            preferred_element_type=jnp.float32,
        ).astype(jnp.bfloat16)
    exchange(win_w, 1)
    for kind in range(3, kinds):
        send_kind(kind)

    base = rank * blocks - RADIUS

    def slot(b, j):
        return jnp.clip(source_in[b, j] - base, 0, win_at.shape[0] - 1)

    chunks = 4
    chunk = members // chunks
    per = chunk // rows
    mine = pl.ds(pl.multiple_of(rank * owned, owned), owned)
    quarter = me // per
    half, odd = quarter // 2, quarter % 2

    def localize(v):
        for b in range(blocks):
            def pair(j, _, b=b):
                covariance = jnp.dot(
                    win_at[slot(b, j)],
                    anom[v, :, b * size : (b + 1) * size],
                    preferred_element_type=jnp.float32,
                )
                local_t[v, b, pl.ds(pl.multiple_of(j * size, size), size), :] = (
                    covariance * taper_t[choice_in[b, j]]
                ).astype(jnp.bfloat16)
                return 0

            lax.fori_loop(0, pairs, pair, 0)

    def answer(v):
        kind = v + 1 if v else 0

        def step(i, _):
            over, flip = i // 2, (i + i // 2) % 2
            at = 2 * (1 - over + (2 * over - 1) * half) + flip + (1 - 2 * flip) * odd
            here = pl.ds(pl.multiple_of(at * chunk, chunk), chunk)
            for b in range(blocks):
                weights = jnp.concatenate(
                    [win_w[slot(b, j), here, :] for j in range(pairs)], axis=1
                )
                increment = jnp.dot(weights, local_t[v, b], preferred_element_type=jnp.float32)
                part_of = slice(b * size, (b + 1) * size)
                outbuf[v, here, part_of] = (
                    rin[kind, here, part_of].astype(jnp.float32) + increment
                ).astype(jnp.bfloat16)

            def give(k, _):
                peer = at * per + lax.rem(k + me, per)
                theirs = pl.ds(pl.multiple_of(peer * rows, rows), rows)

                @pl.when(peer != me)
                def _():
                    pltpu.make_async_remote_copy(
                        src_ref=outbuf.at[v, theirs, :],
                        dst_ref=out.at[v, :, mine],
                        send_sem=out_send,
                        recv_sem=out_recv,
                        device_id=(peer, part),
                        device_id_type=MESH,
                    ).start()

                return 0

            lax.fori_loop(0, per, give, 0)
            return 0

        lax.fori_loop(0, chunks, step, 0)

    for v in range(variables):
        if v:
            arrived(v + 1)
            anom[v] = centered(v + 1)
        else:
            landed(0)
        localize(v)
        if not v:
            landed(1)
        answer(v)

    keep = pltpu.make_async_copy(outbuf.at[:, my_rows, :], out.at[:, :, mine], local_sem.at[kinds + 1])
    keep.start()
    keep.wait()
    for kind in range(kinds):
        block = rin.at[kind, pl.ds(0, remote_rows)]
        pltpu.make_async_copy(block, block, in_send.at[kind]).wait()
    block = outbuf.at[:, pl.ds(0, remote_rows), :]
    pltpu.make_async_copy(block, block, out_send).wait()
    pltpu.make_async_copy(block, block, out_recv).wait()


def on_device(n, state, obs_noise, obs_values, obs_weights, tapers, pair_source, pair_taper):
    variables, rows, cells = state.shape
    members = rows * n
    owned = cells // n
    blocks, size = obs_weights.shape[1], obs_weights.shape[2]
    pairs = pair_source.shape[2]
    window = blocks + 2 * RADIUS
    anywhere = pl.BlockSpec(memory_space=pl.ANY)
    kinds = variables + 1
    return pl.pallas_call(
        functools.partial(kernel, n),
        out_shape=jax.ShapeDtypeStruct(state.shape, state.dtype),
        in_specs=[anywhere] * 7,
        out_specs=anywhere,
        scratch_shapes=[
            pltpu.VMEM((kinds, members, owned), jnp.bfloat16),
            pltpu.VMEM((window, size, members), jnp.bfloat16),
            pltpu.VMEM((window, members, size), jnp.bfloat16),
            pltpu.VMEM((variables, members, owned), jnp.bfloat16),
            pltpu.VMEM((variables, blocks, pairs * size, size), jnp.bfloat16),
            pltpu.VMEM(tapers.shape, jnp.float32),
            pltpu.VMEM(tapers.shape, jnp.float32),
            pltpu.VMEM((variables, members, owned), jnp.bfloat16),
            pltpu.VMEM((blocks, size, size), jnp.bfloat16),
            pltpu.VMEM((1, owned), jnp.float32),
            pltpu.SMEM((blocks, pairs), jnp.int32),
            pltpu.SMEM((blocks, pairs), jnp.int32),
            pltpu.SemaphoreType.DMA((kinds,)),
            pltpu.SemaphoreType.DMA((kinds,)),
            pltpu.SemaphoreType.DMA((kinds + 2,)),
            pltpu.SemaphoreType.DMA((2, 2)),
            pltpu.SemaphoreType.DMA((2, 2)),
            pltpu.SemaphoreType.DMA,
            pltpu.SemaphoreType.DMA,
            pltpu.SemaphoreType.DMA((4,)),
            pltpu.SemaphoreType.DMA((4,)),
        ],
        compiler_params=pltpu.CompilerParams(collective_id=0, has_side_effects=True),
    )(state, obs_noise, obs_values, obs_weights, tapers, pair_source, pair_taper)


def solution(mesh):
    placed = (
        P(None, "mem", "patch"),
        P("mem", "patch"),
        P("patch", "mem"),
        P("patch", "mem", None, None),
        P(),
        P("patch", "mem", None),
        P("patch", "mem", None),
    )
    return jax.shard_map(
        functools.partial(on_device, mesh.shape["mem"]),
        mesh=mesh,
        in_specs=placed,
        out_specs=P(None, "mem", "patch"),
        check_vma=False,
    )
```

time: 123 us -> 98.9 us (0.80)
  the two profiles are of different devices: /device:TPU:29 before, /device:TPU:0 now
where the time goes in v2:
time: 98.9 us; the launch traced here: 98.8 us
  Pallas kernels  96.1 us (97%)
  local copies, waits for them, and re-layouts  2.7 us (3%)
    pallas_call x1, Pallas kernels, on_device(): pl.pallas_call(functools.partial(kernel, n), out_shape=jax.ShapeDtypeStru...  96.1 us
    unnamed x1, local copies, waits for them, and re-layouts  2.7 us

profile of v2, /device:TPU:0, one launch (start us, length us, event | category | flops | bytes accessed | tf_op | source)
XLA Modules:
  0.0 98.8 jit_solution(9607850199711288822)
XLA Ops:
  0.0 96.1 %shard_map.73 = bf16[3,64,4096]{2,1,0:T(8,128)(2,1)} custom-call(bf16[3,64,4096]{2,1,0:T(8,128)(2,1)} %state.1, bf16[64,4096]{1,0:T(8,128)(2,1)} %noise.1, f32[1,256]{1,0:T(1,128)} %obs_values.1, bf16[1,2,128,128]{3,2,1,0:T(8,128)(2,1)} %obs_weights.1, f32[8,128,128]{2,1,0:T(8,128)} %tapers.1, s32[1,2,4]{2,1,0:T(2,128)} %pair_source.1, s32[1,2,4]{2,1,0:T(2,128)} %pair_taper.1), custom_call_target="tpu_custom_call" | custom-call | tf_op jit(solution)/shard_map/pallas_call | solution.py:311
  96.1 2.7 %copy.9 = bf16[3,64,4096]{2,1,0:T(8,128)(2,1)} copy(bf16[3,64,4096]{2,1,0:T(8,128)(2,1)} %shard_map.73) | data formatting | bytes 3145728

commit v3 on v2

--- a/solution.py
+++ b/solution.py
@@ -35,6 +35,7 @@
     out,
     rin, win_at, win_w, anom, local_t, taper_in, taper_t, outbuf, weights_in, values_in, source_in, choice_in,
     in_send, in_recv, local_sem, halo_send, halo_recv, out_send, out_recv, small_send, small_recv,
+    guest_in, guest_weights, guest_values, guest_send, guest_recv, guest_local, guest_small_send, guest_small_recv,
 ):
     me = lax.axis_index("mem")
     part = lax.axis_index("patch")
@@ -44,6 +45,10 @@
     pairs = source_in.shape[1]
     kinds = rin.shape[0]
     rank = rank_of(me, part)
+    low, high = n // 2 - 1, n // 2
+    is_guest = jnp.logical_or(rank == low, rank == high)
+    across = low + high - rank
+    across_start = jnp.where(rank == low, RADIUS + blocks, 0)
 
     barrier = pltpu.get_barrier_semaphore()
 
@@ -68,6 +73,48 @@
     taper_copy = pltpu.make_async_copy(tapers, taper_in, local_sem.at[kinds])
     taper_copy.start()
     pl.semaphore_wait(barrier, n - 1)
+
+    def guest_copy(kind):
+        return pltpu.make_async_copy(
+            source(kind, jnp.clip(across, 0, n - 1)), guest_in.at[kind, my_rows], guest_local.at[kind]
+        )
+
+    def send_guests(kind):
+        for host, other in ((low, high), (high, low)):
+            host_device = device_of(host, part)
+
+            @pl.when(host_device != me)
+            def _():
+                pltpu.make_async_remote_copy(
+                    src_ref=source(kind, other),
+                    dst_ref=guest_in.at[kind, my_rows],
+                    send_sem=guest_send.at[kind],
+                    recv_sem=guest_recv.at[kind],
+                    device_id=(host_device, part),
+                    device_id_type=MESH,
+                ).start()
+
+        @pl.when(is_guest)
+        def _():
+            guest_copy(kind).start()
+
+    guest_small = [(obs_weights.at[0], guest_weights), (obs_values, guest_values)]
+    lends = jnp.logical_or(me == low, me == high)
+
+    def guest_remote(i):
+        return pltpu.make_async_remote_copy(
+            src_ref=guest_small[i][0],
+            dst_ref=guest_small[i][1],
+            send_sem=guest_small_send.at[i],
+            recv_sem=guest_small_recv.at[i],
+            device_id=(device_of(jnp.clip(low + high - me, 0, n - 1), part), part),
+            device_id_type=MESH,
+        )
+
+    def guest_arrived(kind):
+        guest_copy(kind).wait()
+        block = guest_in.at[kind, pl.ds(0, (n - 1) * rows)]
+        pltpu.make_async_copy(block, block, guest_recv.at[kind]).wait()
 
     def send_kind(kind):
         def send(k, _):
@@ -85,6 +132,7 @@
         lax.fori_loop(1, n, send, 0)
 
     send_kind(0)
+    send_guests(0)
     keeper = device_of(me, part)
     small = [
         (obs_weights.at[0], weights_in),
@@ -116,7 +164,13 @@
         for i in range(len(small)):
             small_local(i).start()
 
+    @pl.when(lends)
+    def _():
+        for i in range(len(guest_small)):
+            guest_remote(i).start()
+
     send_kind(1)
+    send_guests(1)
 
     taper_copy.wait()
     for k in range(tapers.shape[0]):
@@ -129,8 +183,8 @@
         block = rin.at[kind, pl.ds(0, remote_rows)]
         pltpu.make_async_copy(block, block, in_recv.at[kind]).wait()
 
-    def centered(kind):
-        values = rin[kind].astype(jnp.float32)
+    def centered(array):
+        values = array.astype(jnp.float32)
         center = jnp.sum(values, axis=0, keepdims=True) * (1.0 / members)
         return (values - center).astype(jnp.bfloat16)
 
@@ -155,11 +209,11 @@
             device_id_type=MESH,
         )
 
-        @pl.when(rank > 0)
+        @pl.when(jnp.logical_and(rank > 0, rank != high))
         def _():
             left.start()
 
-        @pl.when(rank < n - 1)
+        @pl.when(jnp.logical_and(rank < n - 1, rank != low))
         def _():
             right.start()
 
@@ -168,18 +222,18 @@
     def landed(index):
         left, right = halo[index]
 
-        @pl.when(rank > 0)
+        @pl.when(jnp.logical_and(rank > 0, rank != high))
         def _():
             left.wait_send()
             right.wait_recv()
 
-        @pl.when(rank < n - 1)
+        @pl.when(jnp.logical_and(rank < n - 1, rank != low))
         def _():
             right.wait_send()
             left.wait_recv()
 
     arrived(0)
-    first = centered(0)
+    first = centered(rin[0])
     anom[0] = first
     for b in range(blocks):
         win_at[RADIUS + b] = first[:, b * size : (b + 1) * size].T
@@ -197,19 +251,39 @@
             small_local(i).wait()
 
     arrived(1)
-    innovation = (
-        values_in[...] + rin[1].astype(jnp.float32) - rin[0].astype(jnp.float32)
-    ).astype(jnp.bfloat16)
-    for b in range(blocks):
-        win_w[RADIUS + b] = lax.dot_general(
-            innovation[:, b * size : (b + 1) * size],
-            weights_in[b],
-            (((1,), (1,)), ((), ())),
-            preferred_element_type=jnp.float32,
+
+    def weigh(observed, perturbed, values, weights, start):
+        innovation = (
+            values[...] + perturbed.astype(jnp.float32) - observed.astype(jnp.float32)
         ).astype(jnp.bfloat16)
+        for b in range(blocks):
+            win_w[start + b] = lax.dot_general(
+                innovation[:, b * size : (b + 1) * size],
+                weights[b],
+                (((1,), (1,)), ((), ())),
+                preferred_element_type=jnp.float32,
+            ).astype(jnp.bfloat16)
+
+    weigh(rin[0], rin[1], values_in, weights_in, RADIUS)
     exchange(win_w, 1)
     for kind in range(3, kinds):
         send_kind(kind)
+
+    @pl.when(is_guest)
+    def _():
+        guest_arrived(0)
+        values = centered(guest_in[0])
+        for b in range(blocks):
+            win_at[across_start + b] = values[:, b * size : (b + 1) * size].T
+        for i in range(len(guest_small)):
+            guest_remote(i).wait_recv()
+        guest_arrived(1)
+        weigh(guest_in[0], guest_in[1], guest_values, guest_weights, across_start)
+
+    @pl.when(lends)
+    def _():
+        for i in range(len(guest_small)):
+            guest_remote(i).wait_send()
 
     base = rank * blocks - RADIUS
 
@@ -280,7 +354,7 @@
     for v in range(variables):
         if v:
             arrived(v + 1)
-            anom[v] = centered(v + 1)
+            anom[v] = centered(rin[v + 1])
         else:
             landed(0)
         localize(v)
@@ -291,12 +365,58 @@
     keep = pltpu.make_async_copy(outbuf.at[:, my_rows, :], out.at[:, :, mine], local_sem.at[kinds + 1])
     keep.start()
     keep.wait()
+    for kind in range(2):
+        one = guest_in.at[kind, pl.ds(0, rows)]
+        both = guest_in.at[kind, pl.ds(0, 2 * rows)]
+
+        @pl.when(is_guest)
+        def _():
+            pltpu.make_async_copy(one, one, guest_send.at[kind]).wait()
+
+        @pl.when(jnp.logical_not(is_guest))
+        def _():
+            pltpu.make_async_copy(both, both, guest_send.at[kind]).wait()
+
     for kind in range(kinds):
         block = rin.at[kind, pl.ds(0, remote_rows)]
         pltpu.make_async_copy(block, block, in_send.at[kind]).wait()
     block = outbuf.at[:, pl.ds(0, remote_rows), :]
     pltpu.make_async_copy(block, block, out_send).wait()
     pltpu.make_async_copy(block, block, out_recv).wait()
+
+
+def settle(array):
+    parts = 6
+    depth, rows, cells = array.shape
+    width = cells * depth // parts
+
+    def body(given, out, held, came, went):
+        def piece(i):
+            per = parts // depth
+            return i // per, slice(None), pl.ds((i % per) * width, width)
+
+        reads = [pltpu.make_async_copy(given.at[piece(i)], held.at[piece(i)], came.at[i]) for i in range(parts)]
+        writes = [pltpu.make_async_copy(held.at[piece(i)], out.at[piece(i)], went.at[i]) for i in range(parts)]
+        for copy in reads:
+            copy.start()
+        for i in range(parts):
+            reads[i].wait()
+            writes[i].start()
+        for copy in writes:
+            copy.wait()
+
+    anywhere = pl.BlockSpec(memory_space=pl.ANY)
+    return pl.pallas_call(
+        body,
+        out_shape=jax.ShapeDtypeStruct(array.shape, array.dtype),
+        in_specs=[anywhere],
+        out_specs=anywhere,
+        scratch_shapes=[
+            pltpu.VMEM(array.shape, array.dtype),
+            pltpu.SemaphoreType.DMA((parts,)),
+            pltpu.SemaphoreType.DMA((parts,)),
+        ],
+    )(array)
 
 
 def on_device(n, state, obs_noise, obs_values, obs_weights, tapers, pair_source, pair_taper):
@@ -308,7 +428,7 @@
     window = blocks + 2 * RADIUS
     anywhere = pl.BlockSpec(memory_space=pl.ANY)
     kinds = variables + 1
-    return pl.pallas_call(
+    moved = pl.pallas_call(
         functools.partial(kernel, n),
         out_shape=jax.ShapeDtypeStruct(state.shape, state.dtype),
         in_specs=[anywhere] * 7,
@@ -335,9 +455,18 @@
             pltpu.SemaphoreType.DMA,
             pltpu.SemaphoreType.DMA((4,)),
             pltpu.SemaphoreType.DMA((4,)),
+            pltpu.VMEM((2, members, owned), jnp.bfloat16),
+            pltpu.VMEM((blocks, size, size), jnp.bfloat16),
+            pltpu.VMEM((1, owned), jnp.float32),
+            pltpu.SemaphoreType.DMA((2,)),
+            pltpu.SemaphoreType.DMA((2,)),
+            pltpu.SemaphoreType.DMA((2,)),
+            pltpu.SemaphoreType.DMA((2,)),
+            pltpu.SemaphoreType.DMA((2,)),
         ],
         compiler_params=pltpu.CompilerParams(collective_id=0, has_side_effects=True),
     )(state, obs_noise, obs_values, obs_weights, tapers, pair_source, pair_taper)
+    return settle(moved)
 
 
 def solution(mesh):

time: 98.9 us -> 96 us (0.971)
  the two profiles are of different devices: /device:TPU:0 before, /device:TPU:18 now
where the time goes in v3:
time: 96 us; the launch traced here: 95.9 us
  Pallas kernels  95.9 us (100%)
    pallas_call x1, Pallas kernels, on_device(): pl.pallas_call(functools.partial(kernel, n), out_shape=jax.ShapeDtypeStru...  93.7 us
    pallas_call x1, Pallas kernels, settle(): pl.pallas_call(body, out_shape=jax.ShapeDtypeStruct(array.shape, array.dt...  2.19 us

profile of v3, /device:TPU:18, one launch (start us, length us, event | category | flops | bytes accessed | tf_op | source)
XLA Modules:
  0.0 95.9 jit_solution(17976333746473505818)
XLA Ops:
  0.0 93.7 %shard_map.73.given = bf16[3,64,4096]{2,1,0:T(8,128)(2,1)} custom-call(bf16[3,64,4096]{2,1,0:T(8,128)(2,1)} %state.1, bf16[64,4096]{1,0:T(8,128)(2,1)} %noise.1, f32[1,256]{1,0:T(1,128)} %obs_values.1, bf16[1,2,128,128]{3,2,1,0:T(8,128)(2,1)} %obs_weights.1, f32[8,128,128]{2,1,0:T(8,128)} %tapers.1, s32[1,2,4]{2,1,0:T(2,128)} %pair_source.1, ...), custom_call_target="tpu_custom_call" | custom-call | tf_op jit(solution)/shard_map/pallas_call | solution.py:431
  93.7 2.2 %shard_map.74 = bf16[3,64,4096]{2,1,0:T(8,128)(2,1)} custom-call(bf16[3,64,4096]{2,1,0:T(8,128)(2,1)} %shard_map.73.given), custom_call_target="tpu_custom_call" | custom-call | tf_op jit(solution)/shard_map/pallas_call | solution.py:409

commit v4 on v3

--- a/solution.py
+++ b/solution.py
@@ -266,8 +266,6 @@
 
     weigh(rin[0], rin[1], values_in, weights_in, RADIUS)
     exchange(win_w, 1)
-    for kind in range(3, kinds):
-        send_kind(kind)
 
     @pl.when(is_guest)
     def _():
@@ -359,6 +357,8 @@
             landed(0)
         localize(v)
         if not v:
+            for kind in range(3, kinds):
+                send_kind(kind)
             landed(1)
         answer(v)
 

time: 96 us -> 92.9 us (0.968)
  the two profiles are of different devices: /device:TPU:18 before, /device:TPU:0 now
where the time goes in v4:
time: 92.9 us; the launch traced here: 92 us
  Pallas kernels  91.9 us (99%)
    pallas_call x1, Pallas kernels, on_device(): pl.pallas_call(functools.partial(kernel, n), out_shape=jax.ShapeDtypeStru...  89.8 us
    pallas_call x1, Pallas kernels, settle(): pl.pallas_call(body, out_shape=jax.ShapeDtypeStruct(array.shape, array.dt...  2.19 us

profile of v4, /device:TPU:0, one launch (start us, length us, event | category | flops | bytes accessed | tf_op | source)
XLA Modules:
  0.0 92.0 jit_solution(5233147647245383056)
XLA Ops:
  0.0 89.8 %shard_map.73.given = bf16[3,64,4096]{2,1,0:T(8,128)(2,1)} custom-call(bf16[3,64,4096]{2,1,0:T(8,128)(2,1)} %state.1, bf16[64,4096]{1,0:T(8,128)(2,1)} %noise.1, f32[1,256]{1,0:T(1,128)} %obs_values.1, bf16[1,2,128,128]{3,2,1,0:T(8,128)(2,1)} %obs_weights.1, f32[8,128,128]{2,1,0:T(8,128)} %tapers.1, s32[1,2,4]{2,1,0:T(2,128)} %pair_source.1, ...), custom_call_target="tpu_custom_call" | custom-call | tf_op jit(solution)/shard_map/pallas_call | solution.py:431
  89.8 2.2 %shard_map.74 = bf16[3,64,4096]{2,1,0:T(8,128)(2,1)} custom-call(bf16[3,64,4096]{2,1,0:T(8,128)(2,1)} %shard_map.73.given), custom_call_target="tpu_custom_call" | custom-call | tf_op jit(solution)/shard_map/pallas_call | solution.py:409
